TPU v7x, 32 devices: a whole 2x2x4 slice. The times are simulated.
32 devices in a mesh: dp: 8 (over z, core), ctx: 4 (over y, x).
Axes of the slice: x: 2, y: 2, z: 4, core: 2. Of those that a mesh axis runs over, the one named last changes fastest.
Arguments:
- loader_rows: bfloat16 [8192, 512], P(('dp', 'ctx')), may hold values from -60 to 60
- send_slot: int32 [8192], P(('dp', 'ctx')), may hold values from 0 to 383, as said below
- arrive_slot: int32 [8192], P(('dp', 'ctx')), may hold values from 0 to 383, as said below
- user_lengths: int32 [8, 4], P('dp'), may hold values from 1 to 768, 1024 in all within a row
- proj_weight: bfloat16 [512, 2048], replicated, may hold values from -0.25 to 0.25
- out_weight: bfloat16 [512, 512], replicated, may hold values from -0.25 to 0.25
- cotangent: bfloat16 [8192, 512], P(('dp', 'ctx')), may hold values from -6 to 6
Outputs:
- layer_out: bfloat16 [8192, 512], P(('dp', 'ctx'))
- row_grads: bfloat16 [8192, 512], P(('dp', 'ctx'))
- proj_grad: float32 [512, 2048], replicated
- out_grad: float32 [512, 512], replicated
Inputs may be any that keep to these rules, and one draw needn't show every extreme that they name: `send_slot`: on each loader device its 256 entries are distinct slots d * 12 + k, d the owner device and k counting that owner's rows from this loader from 0; no loader sends more than 12 rows to one owner and some pairs send exactly 12; the number of rows from loader s to owner d depends only on (d - s) mod (8 * 4). `arrive_slot`: on each owner device its 256 entries are distinct slots s * 12 + k, the k-th row that loader s sends to it; every owner receives exactly 256 rows.
All inputs are finite; a program needn't handle non-finite values.
Results may differ from a plain program's by a relative error of at most 0.009.
Values may be sent and summed in bfloat16 or wider, within the bound.
No kernel may reach another device: no remote copies, remote signals or barrier semaphores. Data moves between devices by JAX's collectives and lax.ppermute only.
A program may use at most 128 MiB of HBM per device.

v0:
```python
import jax
import jax.numpy as jnp
from jax import lax
from jax.sharding import PartitionSpec as P

HEADS = 8
norm_eps = 1e-05


def normalize(values):
    centre = values - jnp.mean(values, axis=-1, keepdims=True)
    inverse = lax.rsqrt(jnp.mean(centre * centre, axis=-1, keepdims=True) + norm_eps)
    return (centre * inverse, inverse)


def normalize_back(grad_in, normed, inverse):
    mean_grad = jnp.mean(grad_in, axis=-1, keepdims=True)
    mean_cross = jnp.mean(grad_in * normed, axis=-1, keepdims=True)
    return (grad_in - mean_grad - normed * mean_cross) * inverse


def silu_grad(values):
    sigma = jax.nn.sigmoid(values)
    return sigma * (1.0 + values * (1.0 - sigma))


def in_blocks(step_fn, block_rows, running, pieces):
    total_rows = pieces[0].shape[0]

    def one_block(index, carry):
        start = index * block_rows
        sliced = tuple((lax.dynamic_slice_in_dim(each, start, block_rows, 0) for each in pieces))
        return step_fn(carry, sliced, start)

    return lax.fori_loop(0, total_rows // block_rows, one_block, running)


def local(loader_rows, send_slot, arrive_slot, user_lengths, proj_weight, out_weight, cotangent):
    row_count = send_slot.shape[0]
    model_width = out_weight.shape[0]
    head_dim = model_width // HEADS
    score_scale = head_dim ** (-0.5)
    group_size = lax.axis_size("ctx")
    group_count = lax.axis_size("dp")
    device_count = group_size * group_count
    per_pair = row_count // device_count
    capacity = per_pair + max(1, per_pair // 2)
    half_rows = row_count // 2
    group_total = group_size * row_count
    outgoing = (
        jnp.zeros((device_count * capacity, model_width), jnp.bfloat16)
        .at[send_slot]
        .set(loader_rows)
    )
    arrived = lax.all_to_all(
        outgoing.reshape(device_count, capacity, model_width),
        ("dp", "ctx"),
        split_axis=0,
        concat_axis=0,
        tiled=True,
    )
    own_rows = arrived.reshape(device_count * capacity, model_width)[arrive_slot]
    ends = jnp.cumsum(user_lengths[0])

    def position_of(row_index):
        device_of = row_index // row_count
        local_of = row_index % row_count
        return jnp.where(
            local_of < half_rows,
            device_of * half_rows + local_of,
            group_total - (device_of + 1) * half_rows + (local_of - half_rows),
        )

    own_pos = position_of(
        lax.axis_index("ctx") * row_count + jnp.arange(row_count, dtype=jnp.int32)
    )

    def user_of(positions):
        return jnp.sum((ends[None, :] <= positions[:, None]).astype(jnp.int32), axis=1)

    own_users = user_of(own_pos)

    def allowed_of(query_pos, query_users, key_pos, key_users):
        return (key_pos[None, :] <= query_pos[:, None]) & (
            query_users[:, None] == key_users[None, :]
        )

    def split_heads(values):
        return values.reshape(values.shape[0], HEADS, head_dim)

    def merge_heads(values):
        return values.reshape(values.shape[0], model_width)

    def piece_scores(query_part, key_part):
        return (
            jnp.einsum(
                "qhd,khd->hqk",
                split_heads(query_part),
                split_heads(key_part),
                preferred_element_type=jnp.float32,
            )
            * score_scale
        )

    rows_f = own_rows.astype(jnp.float32)
    normed, inverse_in = normalize(rows_f)
    normed_bf = normed.astype(jnp.bfloat16)
    pre = jnp.dot(normed_bf, proj_weight, preferred_element_type=jnp.float32)
    proj = (pre * jax.nn.sigmoid(pre)).astype(jnp.bfloat16)
    update_rows = proj[:, :model_width]
    value_rows = proj[:, model_width : 2 * model_width]
    query_rows = proj[:, 2 * model_width : 3 * model_width]
    key_rows = proj[:, 3 * model_width :]

    def attend_block(running, pieces, first_row):
        key_part, value_part = pieces
        key_pos = position_of(first_row + jnp.arange(key_part.shape[0], dtype=jnp.int32))
        allowed = allowed_of(own_pos, own_users, key_pos, user_of(key_pos))[None]
        scores = piece_scores(query_rows, key_part)
        weights = jnp.where(allowed, scores * jax.nn.sigmoid(scores), 0.0).astype(jnp.bfloat16)
        product = jnp.einsum(
            "hqk,khd->qhd", weights, split_heads(value_part), preferred_element_type=jnp.float32
        )
        return running + merge_heads(product)

    zeros_rows = jnp.zeros((row_count, model_width), jnp.float32)
    attended = in_blocks(
        attend_block,
        row_count,
        zeros_rows,
        (
            lax.all_gather(key_rows, "ctx", axis=0, tiled=True),
            lax.all_gather(value_rows, "ctx", axis=0, tiled=True),
        ),
    )
    att_normed, inverse_att = normalize(attended)
    update_f = update_rows.astype(jnp.float32)
    gated = (att_normed * update_f).astype(jnp.bfloat16)
    layer_rows = (rows_f + jnp.dot(gated, out_weight, preferred_element_type=jnp.float32)).astype(
        jnp.bfloat16
    )
    out_term = jnp.dot(gated.T, cotangent, preferred_element_type=jnp.float32)
    grad_gated = jnp.dot(cotangent, out_weight.T, preferred_element_type=jnp.float32)
    grad_update = grad_gated * att_normed
    grad_att = normalize_back(grad_gated * update_f, att_normed, inverse_att).astype(jnp.bfloat16)

    def query_block(running, pieces, first_row):
        key_part, value_part = pieces
        key_pos = position_of(first_row + jnp.arange(key_part.shape[0], dtype=jnp.int32))
        allowed = allowed_of(own_pos, own_users, key_pos, user_of(key_pos))[None]
        scores = piece_scores(query_rows, key_part)
        grad_weights = jnp.einsum(
            "qhd,khd->hqk",
            split_heads(grad_att),
            split_heads(value_part),
            preferred_element_type=jnp.float32,
        )
        grad_scores = jnp.where(
            allowed, grad_weights * silu_grad(scores) * score_scale, 0.0
        ).astype(jnp.bfloat16)
        product = jnp.einsum(
            "hqk,khd->qhd", grad_scores, split_heads(key_part), preferred_element_type=jnp.float32
        )
        return running + merge_heads(product)

    def key_block(running, pieces, first_row):
        query_part, grad_part = pieces
        query_pos = position_of(first_row + jnp.arange(query_part.shape[0], dtype=jnp.int32))
        allowed = allowed_of(query_pos, user_of(query_pos), own_pos, own_users)[None]
        scores = piece_scores(query_part, key_rows)
        weights = jnp.where(allowed, scores * jax.nn.sigmoid(scores), 0.0).astype(jnp.bfloat16)
        grad_weights = jnp.einsum(
            "qhd,khd->hqk",
            split_heads(grad_part),
            split_heads(value_rows),
            preferred_element_type=jnp.float32,
        )
        grad_scores = jnp.where(
            allowed, grad_weights * silu_grad(scores) * score_scale, 0.0
        ).astype(jnp.bfloat16)
        grad_key = jnp.einsum(
            "hqk,qhd->khd", grad_scores, split_heads(query_part), preferred_element_type=jnp.float32
        )
        grad_value = jnp.einsum(
            "hqk,qhd->khd", weights, split_heads(grad_part), preferred_element_type=jnp.float32
        )
        return (running[0] + merge_heads(grad_key), running[1] + merge_heads(grad_value))

    grad_query = in_blocks(
        query_block,
        row_count,
        zeros_rows,
        (
            lax.all_gather(key_rows, "ctx", axis=0, tiled=True),
            lax.all_gather(value_rows, "ctx", axis=0, tiled=True),
        ),
    )
    grad_key, grad_value = in_blocks(
        key_block,
        row_count,
        (zeros_rows, zeros_rows),
        (
            lax.all_gather(query_rows, "ctx", axis=0, tiled=True),
            lax.all_gather(grad_att, "ctx", axis=0, tiled=True),
        ),
    )
    grad_proj = jnp.concatenate([grad_update, grad_value, grad_query, grad_key], axis=1)
    grad_pre = (grad_proj * silu_grad(pre)).astype(jnp.bfloat16)
    proj_term = jnp.dot(normed_bf.T, grad_pre, preferred_element_type=jnp.float32)
    grad_normed = jnp.dot(grad_pre, proj_weight.T, preferred_element_type=jnp.float32)
    row_grads = (
        cotangent.astype(jnp.float32) + normalize_back(grad_normed, normed, inverse_in)
    ).astype(jnp.bfloat16)
    proj_sum, out_sum = lax.psum((proj_term, out_term), ("dp", "ctx"))
    grad_scale = (row_count * device_count) ** (-0.5)
    return (layer_rows, row_grads, proj_sum * grad_scale, out_sum * grad_scale)


def solution(mesh):
    placed = (
        P(("dp", "ctx"), None),
        P(("dp", "ctx")),
        P(("dp", "ctx")),
        P("dp", None),
        P(),
        P(),
        P(("dp", "ctx"), None),
    )
    return jax.shard_map(
        local,
        mesh=mesh,
        in_specs=placed,
        out_specs=(P(("dp", "ctx"), None), P(("dp", "ctx"), None), P(), P()),
        check_vma=False,
    )
```

profile of v0, /device:TPU:0, one launch (start us, length us, event | category | flops | bytes accessed | tf_op | source)
XLA Modules:
  0.0 400.7 jit_solution(9366824799308477023)
XLA Ops:
  8.0 2.0 scatter_custom_fusion
  10.9 7.3 %all-to-all-start = ((bf16[32,12,512]{2,1,0:T(8,128)(2,1)}), bf16[32,12,512]{2,1,0:T(8,128)(2,1)S(1)}, u32[]{:S(2)}, u32[]{:S(2)}) async-start(bf16[32,12,512]{2,1,0:T(8,128)(2,1)} %reshape.616), calls=%async_computation | async-start | bytes 1048576 | tf_op jit(solution)/shard_map/all_to_all | solution.py:55
  18.4 16.2 %all-to-all-done = bf16[32,12,512]{2,1,0:T(8,128)(2,1)S(1)} async-done(((bf16[32,12,512]{2,1,0:T(8,128)(2,1)}), bf16[32,12,512]{2,1,0:T(8,128)(2,1)S(1)}, u32[]{:S(2)}, u32[]{:S(2)}) %all-to-all-start) | async-done | bytes 393248 | tf_op jit(solution)/shard_map/all_to_all | solution.py:55
  36.2 2.1 multiply_convert_fusion
  45.8 18.7 %all-gather.5.cloned.1.call-done = bf16[1024,512]{1,0:T(8,128)(2,1)} async-done(((bf16[256,512]{1,0:T(8,128)(2,1)}), bf16[1024,512]{1,0:T(8,128)(2,1)}) %all-gather.5.cloned.1.call-update) | async-done | bytes 1048592 | tf_op jit(solution)/shard_map/all_gather | solution.py:133
  64.5 2.3 copy.48
  66.8 26.7 %all-gather.7.cloned.1.call-done = bf16[1024,512]{1,0:T(8,128)(2,1)} async-done(((bf16[256,512]{1,0:T(8,128)(2,1)}), bf16[1024,512]{1,0:T(8,128)(2,1)}) %all-gather.7.cloned.1.call-update) | async-done | bytes 1048592 | tf_op jit(solution)/shard_map/all_gather | solution.py:132
  93.5 2.3 copy.49
  95.7 17.4 %while.50 = (s32[]{:T(128)}, f32[256,512]{0,1:T(8,128)S(1)}, bf16[1024,512]{0,1:T(8,128)(2,1)}, s32[256]{0:T(256)S(1)}, s32[4]{0:T(128)S(1)}, /*index=5*/bf16[10...) while((s32[]{:T(128)}, f32[256,512]{0,1:T(8,128)S(1)}, ...), condition=%wide.region_7.8_spmd.clone, body=%wide.region_5.7_spmd.clone.sunk | while | flops 138364160 | bytes 4071625 | solution.py:35
  97.9 2.1 fusion.118
  102.2 2.1 fusion.118
  106.6 2.1 fusion.118
  111.0 2.1 fusion.118
  115.4 2.1 multiply_convert_fusion.1
  118.6 46.4 %while.52 = (s32[]{:T(128)}, f32[256,512]{0,1:T(8,128)}, bf16[1024,512]{0,1:T(8,128)(2,1)}, s32[256]{0:T(256)S(1)}, s32[4]{0:T(128)S(1)}, /*index=5*/bf16[1024,5...) while((s32[]{:T(128)}, f32[256,512]{0,1:T(8,128)}, ...), condition=%wide.region_17.18_spmd.clone, body=%wide.region_15.17_spmd.clone.sunk | while | flops 208094464 | bytes 12984529 | solution.py:35
  119.9 3.2 fusion.133
  123.2 2.9 copy.73
  126.0 2.3 fusion.134
  130.7 3.2 fusion.133
  133.9 2.9 copy.73
  136.8 2.3 fusion.134
  142.7 3.2 fusion.133
  145.9 2.9 copy.73
  148.8 2.3 fusion.134
  154.5 3.2 fusion.133
  157.7 2.9 copy.73
  160.6 2.3 fusion.134
  164.9 2.1 copy.61
  167.0 2.3 fusion.70
  169.4 61.8 %while.51 = (s32[]{:T(128)}, f32[256,512]{0,1:T(8,128)S(1)}, f32[256,512]{0,1:T(8,128)}, bf16[1024,512]{1,0:T(8,128)(2,1)}, s32[4]{0:T(128)S(1)}, /*index=5*/s32...) while((s32[]{:T(128)}, f32[256,512]{0,1:T(8,128)S(1)}, ...), condition=%wide.region_14.15_spmd.clone, body=%wide.region_12.14_spmd.clone.sunk | while | flops 279135488 | bytes 18555156 | solution.py:35
  170.5 2.8 fusion.125
  175.4 3.8 fusion.127
  179.2 3.3 fusion.126
  185.9 2.8 fusion.125
  190.8 3.8 fusion.127
  194.6 3.3 fusion.126
  201.4 2.8 fusion.125
  206.2 3.8 fusion.127
  210.0 3.3 fusion.126
  216.8 2.8 fusion.125
  221.7 3.8 fusion.127
  225.5 3.3 fusion.126
  231.1 2.1 copy.60
  234.2 3.0 fusion.45
  237.2 2.9 fusion.63
  240.1 2.1 fusion.46
  244.1 144.0 %all-reduce.3.cloned.1.call-done = (f32[512,2048]{1,0:T(8,128)}, f32[512,512]{1,0:T(8,128)}) async-done(((f32[512,2048]{1,0:T(8,128)}, f32[512,512]{1,0:T(8,128)}), (f32[512,2048]{1,0:T(8,128)}, f32[512,512]{1,0:T(8,128)})) %all-reduce.3.cloned.1.call-update) | async-done | bytes 5242896 | tf_op jit(solution)/shard_map/psum | solution.py:214
  388.1 5.0 %broadcast_multiply_fusion = f32[512,2048]{1,0:T(8,128)} fusion(f32[512,2048]{1,0:T(8,128)} %get-tuple-element.919), kind=kLoop, calls=%fused_computation.106 | loop fusion | flops 1048576 | bytes 8388608 | tf_op jit(solution)/shard_map/mul | solution.py:216
  (157 shorter events, 61.4 us)
Async XLA Ops:
  7.2 29.0 %copy-start = (bf16[512,2048]{1,0:T(8,128)(2,1)S(1)}, bf16[512,2048]{1,0:T(8,128)(2,1)}, u32[]{:S(2)}) copy-start(bf16[512,2048]{1,0:T(8,128)(2,1)} %param.17) | copy-start | bytes 6291460
  7.2 11.1 %copy-start.9 = (s32[256]{0:T(256)S(1)}, s32[256]{0:T(256)}, u32[]{:S(2)}) copy-start(s32[256]{0:T(256)} %param.15) | copy-start | bytes 3076
  10.9 23.6 %all-to-all-start = ((bf16[32,12,512]{2,1,0:T(8,128)(2,1)}), bf16[32,12,512]{2,1,0:T(8,128)(2,1)S(1)}, u32[]{:S(2)}, u32[]{:S(2)}) async-start(bf16[32,12,512]{2,1,0:T(8,128)(2,1)} %reshape.616), calls=%async_computation | async-start | bytes 1048576 | tf_op jit(solution)/shard_map/all_to_all | solution.py:55
  18.3 46.2 %all-gather.5.cloned.1.call-start = ((), (), s32[]{:S(2)}) async-start(), calls=%async_computation.1 | async-start | bytes 1310720 | tf_op jit(solution)/shard_map/all_gather | solution.py:133
  38.3 1.0 copy-start.7
  38.3 2.7 copy-start.10
  40.1 5.6 %copy-start.5 = (bf16[256,512]{1,0:T(8,128)(2,1)}, bf16[256,512]{1,0:T(8,128)(2,1)S(1)}, u32[]{:S(2)}) copy-start(bf16[256,512]{1,0:T(8,128)(2,1)S(1)} %get-tuple-element.934) | copy-start | bytes 786436
  40.2 53.3 %all-gather.7.cloned.1.call-start = ((), (), s32[]{:S(2)}) async-start(), calls=%async_computation.2 | async-start | bytes 1310720 | tf_op jit(solution)/shard_map/all_gather | solution.py:132
  40.9 128.5 %all-gather.9.cloned.1.call-start = ((), (), s32[]{:S(2)}) async-start(), calls=%async_computation.3 | async-start | bytes 1310720 | tf_op jit(solution)/shard_map/all_gather | solution.py:203
  45.8 123.6 %all-gather.11.cloned.1.call-start = ((), (), s32[]{:S(2)}) async-start(), calls=%async_computation.4 | async-start | bytes 1310720 | tf_op jit(solution)/shard_map/all_gather | solution.py:204
  117.5 0.8 copy-start.4
  118.3 269.8 %all-reduce.3.cloned.1.call-start = ((), (), s32[]{:S(2)}) async-start(), calls=%async_computation.5 | async-start | bytes 10485760 | tf_op jit(solution)/shard_map/psum | solution.py:214
  164.9 4.4 %copy-start.1 = (f32[256,512]{0,1:T(8,128)S(1)}, f32[256,512]{0,1:T(8,128)}, u32[]{:S(2)}) copy-start(f32[256,512]{0,1:T(8,128)} %custom-call.1) | copy-start | bytes 1572868
  179.2 3.3 copy-start.2
  184.0 0.8 copy-start.3
  194.6 3.3 copy-start.2
  199.4 0.8 copy-start.3
  210.0 3.3 copy-start.2
  214.9 0.8 copy-start.3
  225.5 3.3 copy-start.2
  230.3 0.8 copy-start.3
  242.2 0.9 copy-start.6
  388.1 5.0 %copy-start.8 = (f32[512,512]{1,0:T(8,128)S(1)}, f32[512,512]{1,0:T(8,128)}, u32[]{:S(2)}) copy-start(f32[512,512]{1,0:T(8,128)} %get-tuple-element.920) | copy-start | bytes 3145732
Sparse Core Ops, SparseCore 0:
  40.3 24.1 all-gather.4
  66.9 26.4 all-gather.6
  95.3 26.5 all-gather.8
  123.6 26.4 all-gather.10
  240.2 147.8 all-reduce.2
where the time goes:
time: 403 us; the launch traced here: 401 us
  waiting for transfers between devices  206 us (51%)
  matrix products  82.1 us (20%)
  local copies, waits for them, and re-layouts  59.7 us (15%)
  other arithmetic  30.5 us (8%)
  between operations  14 us (3%)
  starting transfers between devices  7.71 us (2%)
    psum x1, waiting for transfers between devices, local(): proj_sum, out_sum = lax.psum((proj_term, out_term), ('dp', 'ctx'))  144 us
    all_gather x1, waiting for transfers between devices, local(): lax.all_gather(key_rows, 'ctx', axis=0, tiled=True)  26.7 us
    dot_general x8, matrix products, piece_scores(): jnp.einsum('qhd,khd->hqk', split_heads(query_part), split_heads(key_part)...  24.1 us
    dynamic_slice x24, local copies, waits for them, and re-layouts, one_block(): lax.dynamic_slice_in_dim(each, start, block_rows, 0)  23.5 us
    all_gather x1, waiting for transfers between devices, local(): lax.all_gather(value_rows, 'ctx', axis=0, tiled=True)  18.7 us
    all_to_all x1, waiting for transfers between devices, local(): lax.all_to_all(outgoing.reshape(device_count, capacity, model_width), ('d...  16.2 us
    dot_general x4, matrix products, key_block(): jnp.einsum('hqk,qhd->khd', grad_scores, split_heads(query_part), preferre...  15.2 us
    dot_general x4, matrix products, key_block(): jnp.einsum('hqk,qhd->khd', weights, split_heads(grad_part), preferred_ele...  13.1 us
  transfers between devices with their start and end apart: 6, of which 4 were waited for; matrix products, arithmetic and copies ran while one was open for 22% of the time, Pallas kernels for 0%

commit v1 on v0

--- a/solution.py
+++ b/solution.py
@@ -5,6 +5,11 @@
 
 HEADS = 8
 norm_eps = 1e-05
+
+
+def by_each_axis(array, first, second):
+    partial = lax.psum(array, first)
+    return lax.psum(partial, second)
 
 
 def normalize(values):
@@ -211,7 +216,7 @@
     row_grads = (
         cotangent.astype(jnp.float32) + normalize_back(grad_normed, normed, inverse_in)
     ).astype(jnp.bfloat16)
-    proj_sum, out_sum = lax.psum((proj_term, out_term), ("dp", "ctx"))
+    proj_sum, out_sum = by_each_axis((proj_term, out_term), "ctx", "dp")
     grad_scale = (row_count * device_count) ** (-0.5)
     return (layer_rows, row_grads, proj_sum * grad_scale, out_sum * grad_scale)
 

time: 403 us -> 494 us (1.23)
  waiting for transfers between devices: 206 us -> 298 us
    psum x1 -> x2, waiting for transfers between devices: 144 us -> 236 us  [the longest x1 121 us: by_each_axis(): partial = lax.psum(array, first)]
  transfers between devices with their start and end apart: 6 -> 7, of which waited for: 4 -> 5; matrix products, arithmetic and copies ran while one was open for 22% -> 17% of each run, Pallas kernels for 0% -> 0%
where the time goes in v1:
time: 494 us; the launch traced here: 492 us
  waiting for transfers between devices  298 us (60%)
  matrix products  81.9 us (17%)
  local copies, waits for them, and re-layouts  59.6 us (12%)
  other arithmetic  30.4 us (6%)
  between operations  14.3 us (3%)
  starting transfers between devices  7.75 us (2%)
    psum x1, waiting for transfers between devices, by_each_axis(): partial = lax.psum(array, first)  121 us
    psum x1, waiting for transfers between devices, by_each_axis(): return lax.psum(partial, second)  115 us
    all_gather x1, waiting for transfers between devices, local(): lax.all_gather(key_rows, 'ctx', axis=0, tiled=True)  26.7 us
    dot_general x8, matrix products, piece_scores(): jnp.einsum('qhd,khd->hqk', split_heads(query_part), split_heads(key_part)...  24 us
    dynamic_slice x24, local copies, waits for them, and re-layouts, one_block(): lax.dynamic_slice_in_dim(each, start, block_rows, 0)  23.5 us
    all_gather x1, waiting for transfers between devices, local(): lax.all_gather(value_rows, 'ctx', axis=0, tiled=True)  18.7 us
    all_to_all x1, waiting for transfers between devices, local(): lax.all_to_all(outgoing.reshape(device_count, capacity, model_width), ('d...  16.2 us
    dot_general x4, matrix products, key_block(): jnp.einsum('hqk,qhd->khd', grad_scores, split_heads(query_part), preferre...  15.2 us
  transfers between devices with their start and end apart: 7, of which 5 were waited for; matrix products, arithmetic and copies ran while one was open for 17% of the time, Pallas kernels for 0%

profile of v1, /device:TPU:0, one launch (start us, length us, event | category | flops | bytes accessed | tf_op | source)
XLA Modules:
  0.0 492.4 jit_solution(10365841640873411393)
XLA Ops:
  10.9 7.3 %all-to-all-start = ((bf16[32,12,512]{2,1,0:T(8,128)(2,1)}), bf16[32,12,512]{2,1,0:T(8,128)(2,1)S(1)}, u32[]{:S(2)}, u32[]{:S(2)}) async-start(bf16[32,12,512]{2,1,0:T(8,128)(2,1)} %reshape.616), calls=%async_computation | async-start | bytes 1048576 | tf_op jit(solution)/shard_map/all_to_all | solution.py:60
  18.4 16.2 %all-to-all-done = bf16[32,12,512]{2,1,0:T(8,128)(2,1)S(1)} async-done(((bf16[32,12,512]{2,1,0:T(8,128)(2,1)}), bf16[32,12,512]{2,1,0:T(8,128)(2,1)S(1)}, u32[]{:S(2)}, u32[]{:S(2)}) %all-to-all-start) | async-done | bytes 393248 | tf_op jit(solution)/shard_map/all_to_all | solution.py:60
  36.2 2.1 multiply_convert_fusion
  45.8 18.7 %all-gather.5.cloned.1.call-done = bf16[1024,512]{1,0:T(8,128)(2,1)} async-done(((bf16[256,512]{1,0:T(8,128)(2,1)}), bf16[1024,512]{1,0:T(8,128)(2,1)}) %all-gather.5.cloned.1.call-update) | async-done | bytes 1048592 | tf_op jit(solution)/shard_map/all_gather | solution.py:138
  64.5 2.3 copy.48
  66.8 26.7 %all-gather.7.cloned.1.call-done = bf16[1024,512]{1,0:T(8,128)(2,1)} async-done(((bf16[256,512]{1,0:T(8,128)(2,1)}), bf16[1024,512]{1,0:T(8,128)(2,1)}) %all-gather.7.cloned.1.call-update) | async-done | bytes 1048592 | tf_op jit(solution)/shard_map/all_gather | solution.py:137
  93.4 2.3 copy.49
  95.7 17.4 %while.50 = (s32[]{:T(128)}, f32[256,512]{0,1:T(8,128)S(1)}, bf16[1024,512]{0,1:T(8,128)(2,1)}, s32[256]{0:T(256)S(1)}, s32[4]{0:T(128)S(1)}, /*index=5*/bf16[10...) while((s32[]{:T(128)}, f32[256,512]{0,1:T(8,128)S(1)}, ...), condition=%wide.region_7.8_spmd.clone, body=%wide.region_5.7_spmd.clone.sunk | while | flops 138364160 | bytes 4071625 | solution.py:40
  97.8 2.1 fusion.118
  102.2 2.1 fusion.118
  106.6 2.1 fusion.118
  110.9 2.1 fusion.118
  115.3 2.1 multiply_convert_fusion.1
  118.5 46.2 %while.52 = (s32[]{:T(128)}, f32[256,512]{0,1:T(8,128)}, bf16[1024,512]{0,1:T(8,128)(2,1)}, s32[256]{0:T(256)S(1)}, s32[4]{0:T(128)S(1)}, /*index=5*/bf16[1024,5...) while((s32[]{:T(128)}, f32[256,512]{0,1:T(8,128)}, ...), condition=%wide.region_17.18_spmd.clone, body=%wide.region_15.17_spmd.clone.sunk | while | flops 208094464 | bytes 12984529 | solution.py:40
  119.9 3.2 fusion.133
  123.1 2.9 copy.73
  126.0 2.3 fusion.134
  130.6 3.2 fusion.133
  133.9 2.9 copy.73
  136.7 2.3 fusion.134
  142.5 3.2 fusion.133
  145.8 2.9 copy.73
  148.6 2.3 fusion.134
  154.3 3.2 fusion.133
  157.5 2.9 copy.73
  160.4 2.3 fusion.134
  164.7 2.1 copy.61
  166.8 2.3 fusion.70
  169.2 61.7 %while.51 = (s32[]{:T(128)}, f32[256,512]{0,1:T(8,128)S(1)}, f32[256,512]{0,1:T(8,128)}, bf16[1024,512]{1,0:T(8,128)(2,1)}, s32[4]{0:T(128)S(1)}, /*index=5*/s32...) while((s32[]{:T(128)}, f32[256,512]{0,1:T(8,128)S(1)}, ...), condition=%wide.region_14.15_spmd.clone, body=%wide.region_12.14_spmd.clone.sunk | while | flops 279135488 | bytes 18555156 | solution.py:40
  170.3 2.8 fusion.125
  175.1 3.8 fusion.127
  178.9 3.3 fusion.126
  185.7 2.8 fusion.125
  190.6 3.8 fusion.127
  194.4 3.3 fusion.126
  201.1 2.8 fusion.125
  206.0 3.8 fusion.127
  209.8 3.3 fusion.126
  216.6 2.8 fusion.125
  221.4 3.8 fusion.127
  225.2 3.3 fusion.126
  230.9 2.0 copy.60
  233.9 3.0 fusion.45
  236.9 2.9 fusion.63
  239.8 121.0 %all-reduce.7.cloned.1.call-done = (f32[512,2048]{1,0:T(8,128)}, f32[512,512]{1,0:T(8,128)}) async-done(((f32[512,2048]{1,0:T(8,128)}, f32[512,512]{1,0:T(8,128)}), (f32[512,2048]{1,0:T(8,128)}, f32[512,512]{1,0:T(8,128)})) %all-reduce.7.cloned.1.call-update) | async-done | bytes 5242896 | tf_op jit(solution)/shard_map/psum | solution.py:11
  360.9 2.1 fusion.46
  364.9 114.5 %all-reduce.5.cloned.1.call-done = (f32[512,2048]{1,0:T(8,128)}, f32[512,512]{1,0:T(8,128)}) async-done(((f32[512,2048]{1,0:T(8,128)}, f32[512,512]{1,0:T(8,128)}), (f32[512,2048]{1,0:T(8,128)}, f32[512,512]{1,0:T(8,128)})) %all-reduce.5.cloned.1.call-update) | async-done | bytes 5242896 | tf_op jit(solution)/shard_map/psum | solution.py:12
  479.5 5.0 %broadcast_multiply_fusion = f32[512,2048]{1,0:T(8,128)} fusion(f32[512,2048]{1,0:T(8,128)} %get-tuple-element.919), kind=kLoop, calls=%fused_computation.106 | loop fusion | flops 1048576 | bytes 8388608 | tf_op jit(solution)/shard_map/mul | solution.py:221
  (160 shorter events, 63.4 us)
Async XLA Ops:
  7.2 29.0 %copy-start = (bf16[512,2048]{1,0:T(8,128)(2,1)S(1)}, bf16[512,2048]{1,0:T(8,128)(2,1)}, u32[]{:S(2)}) copy-start(bf16[512,2048]{1,0:T(8,128)(2,1)} %param.17) | copy-start | bytes 6291460
  7.2 11.1 %copy-start.9 = (s32[256]{0:T(256)S(1)}, s32[256]{0:T(256)}, u32[]{:S(2)}) copy-start(s32[256]{0:T(256)} %param.15) | copy-start | bytes 3076
  10.9 23.6 %all-to-all-start = ((bf16[32,12,512]{2,1,0:T(8,128)(2,1)}), bf16[32,12,512]{2,1,0:T(8,128)(2,1)S(1)}, u32[]{:S(2)}, u32[]{:S(2)}) async-start(bf16[32,12,512]{2,1,0:T(8,128)(2,1)} %reshape.616), calls=%async_computation | async-start | bytes 1048576 | tf_op jit(solution)/shard_map/all_to_all | solution.py:60
  18.3 46.2 %all-gather.5.cloned.1.call-start = ((), (), s32[]{:S(2)}) async-start(), calls=%async_computation.1 | async-start | bytes 1310720 | tf_op jit(solution)/shard_map/all_gather | solution.py:138
  38.3 1.0 copy-start.7
  38.3 2.7 copy-start.10
  40.1 5.6 %copy-start.5 = (bf16[256,512]{1,0:T(8,128)(2,1)}, bf16[256,512]{1,0:T(8,128)(2,1)S(1)}, u32[]{:S(2)}) copy-start(bf16[256,512]{1,0:T(8,128)(2,1)S(1)} %get-tuple-element.936) | copy-start | bytes 786436
  40.1 53.3 %all-gather.7.cloned.1.call-start = ((), (), s32[]{:S(2)}) async-start(), calls=%async_computation.2 | async-start | bytes 1310720 | tf_op jit(solution)/shard_map/all_gather | solution.py:137
  40.9 128.3 %all-gather.9.cloned.1.call-start = ((), (), s32[]{:S(2)}) async-start(), calls=%async_computation.3 | async-start | bytes 1310720 | tf_op jit(solution)/shard_map/all_gather | solution.py:208
  45.7 123.5 %all-gather.11.cloned.1.call-start = ((), (), s32[]{:S(2)}) async-start(), calls=%async_computation.4 | async-start | bytes 1310720 | tf_op jit(solution)/shard_map/all_gather | solution.py:209
  117.4 0.8 copy-start.4
  118.3 242.6 %all-reduce.7.cloned.1.call-start = ((), (), s32[]{:S(2)}) async-start(), calls=%async_computation.6 | async-start | bytes 10485760 | tf_op jit(solution)/shard_map/psum | solution.py:11
  164.7 4.4 copy-start.1
  178.9 3.3 copy-start.2
  183.8 0.8 copy-start.3
  194.4 3.3 copy-start.2
  199.2 0.8 copy-start.3
  209.8 3.3 copy-start.2
  214.6 0.8 copy-start.3
  225.2 3.3 copy-start.2
  230.0 0.8 copy-start.3
  239.8 239.7 %all-reduce.5.cloned.1.call-start = ((), (), s32[]{:S(2)}) async-start(), calls=%async_computation.5 | async-start | bytes 10485760 | tf_op jit(solution)/shard_map/psum | solution.py:12
  363.0 0.9 copy-start.6
  479.5 5.0 %copy-start.8 = (f32[512,512]{1,0:T(8,128)S(1)}, f32[512,512]{1,0:T(8,128)}, u32[]{:S(2)}) copy-start(f32[512,512]{1,0:T(8,128)} %get-tuple-element.920) | copy-start | bytes 3145732
Sparse Core Ops, SparseCore 0:
  40.3 24.1 all-gather.4
  66.9 26.4 all-gather.6
  95.3 26.5 all-gather.8
  123.5 26.4 all-gather.10
  239.9 120.9 all-reduce.6
  363.2 116.2 all-reduce.4
